TPU v7x, 32 devices: a whole 2x2x4 slice. The times are simulated.
32 devices in a mesh: section: 2 (over x), expert: 4 (over z), shard: 4 (over y, core).
Axes of the slice: x: 2, y: 2, z: 4, core: 2. Of those that a mesh axis runs over, the one named last changes fastest.
Arguments:
- fwd_in: bfloat16 [2, 512, 3584], P('section', 'expert', 'shard'), may hold values from -6 to 6
- saved_in: bfloat16 [2, 512, 3584], P('section', 'expert', 'shard'), may hold values from -6 to 6
- grad_in: bfloat16 [2, 512, 3584], P('section', 'expert', 'shard'), may hold values from -6 to 6
- w_in: bfloat16 [2, 4, 3584, 1024], P('section', 'expert', 'shard'), may hold values from -0.09375 to 0.09375
- w_out: bfloat16 [2, 4, 1024, 3584], P('section', 'expert', None, 'shard'), may hold values from -0.1875 to 0.1875
- ids_fwd: int32 [2, 512, 2], P('section', 'expert'), may hold values from 0 to 3, all different within a row; in each aligned block of 128 rows (0 to 127, 128 to 255, ..., all dimensions but the last counted through in order) at most 80 rows name the same one
- weight_fwd: int32 [2, 512, 2], P('section', 'expert'), may hold values from 3277 to 65535
- ids_bwd: int32 [2, 512, 2], P('section', 'expert'), may hold values from 0 to 3, all different within a row; in each aligned block of 128 rows (0 to 127, 128 to 255, ..., all dimensions but the last counted through in order) at most 80 rows name the same one
- weight_bwd: int32 [2, 512, 2], P('section', 'expert'), may hold values from 3277 to 65535
Outputs:
- fwd_out: bfloat16 [2, 512, 3584], P('section', 'expert', 'shard')
- bwd_out: bfloat16 [2, 512, 3584], P('section', 'expert', 'shard')
Inputs may be any that keep to these rules, and one draw needn't show every extreme that they name: `ids_fwd`: the 2 experts of a token differ. In each layer, among the 128 tokens of one index of the expert axis, no expert is chosen by more than 80 slots. `ids_bwd`: the 2 experts of a token differ. In each layer, among the 128 tokens of one index of the expert axis, no expert is chosen by more than 80 slots.
All inputs are finite; a program needn't handle non-finite values.
Results may differ from a plain program's by a relative error of at most 0.0049.
Values may be sent and summed in bfloat16 or wider, within the bound.
A program may use at most 64 MiB of HBM per device.

v0:
```python
import jax
import jax.numpy as jnp
from jax import lax
from jax.sharding import PartitionSpec as P


def from_behind(value, axis, steps):
    count = lax.axis_size(axis)
    pairs = [(source, (source + steps) % count) for source in range(count)]
    return lax.ppermute(value, axis, pairs)


def destinations(route_ids, experts, capacity):
    tokens, slot_count = route_ids.shape
    flat_ids = route_ids.reshape(-1)
    labels = jnp.arange(experts, dtype=jnp.int32)
    onehot = (flat_ids[:, None] == labels[None, :]).astype(jnp.int32)
    before = jnp.cumsum(onehot, axis=0) - onehot
    ranking = jnp.sum(before * onehot, axis=1)
    return (flat_ids * capacity + ranking).reshape(tokens, slot_count)


def dispatch_matrix(targets, slot_total):
    labels = jnp.arange(slot_total, dtype=jnp.int32)
    hits = jnp.zeros((slot_total, targets.shape[0]), jnp.float32)
    for column in range(targets.shape[1]):
        hits = hits + (labels[:, None] == targets[None, :, column]).astype(jnp.float32)
    return hits.astype(jnp.bfloat16)


def by_expert(received, expert_group, local_experts, capacity):
    features = received.shape[-1]
    shaped = received.reshape(expert_group, local_experts, capacity, features)
    return shaped.transpose(1, 0, 2, 3).reshape(local_experts, expert_group * capacity, features)


def by_source(results, expert_group, local_experts, capacity):
    features = results.shape[-1]
    shaped = results.reshape(local_experts, expert_group, capacity, features)
    return shaped.transpose(1, 0, 2, 3).reshape(expert_group * local_experts * capacity, features)


def mix_rows(tok_rows, targets, route_weight, returned):
    picked = returned[targets].astype(jnp.float32)
    slot_weight = route_weight.astype(jnp.float32) / 32768.0
    summed = jnp.sum(slot_weight[:, :, None] * picked, axis=1)
    return (tok_rows.astype(jnp.float32) + summed).astype(jnp.bfloat16)


def per_device(fwd_in, saved_in, grad_in, w_in, w_out, ids_fwd, weight_fwd, ids_bwd, weight_bwd):
    expert_group = lax.axis_size("expert")
    local_experts = w_in.shape[1]
    experts = expert_group * local_experts
    tok_count = fwd_in.shape[1]
    slot_count = ids_fwd.shape[2]
    capacity = max(2, (tok_count * slot_count * 5 + 4 * experts - 1) // (4 * experts))
    slot_total = experts * capacity
    up_local = w_in[0]
    down_local = w_out[0]
    fwd_rows = fwd_in[0]
    saved_rows = saved_in[0]
    grad_rows = grad_in[0]
    fwd_targets = destinations(ids_fwd[0], experts, capacity)
    fwd_picker = dispatch_matrix(fwd_targets, slot_total)
    fwd_packed = jnp.dot(fwd_picker, fwd_rows, preferred_element_type=jnp.float32).astype(
        jnp.bfloat16
    )
    fwd_received = lax.all_to_all(fwd_packed, "expert", split_axis=0, concat_axis=0, tiled=True)
    fwd_slots = by_expert(fwd_received, expert_group, local_experts, capacity)
    bwd_targets = destinations(ids_bwd[0], experts, capacity)
    bwd_picker = dispatch_matrix(bwd_targets, slot_total)
    bwd_packed = jnp.dot(bwd_picker, saved_rows, preferred_element_type=jnp.float32).astype(
        jnp.bfloat16
    )
    grad_packed = jnp.dot(bwd_picker, grad_rows, preferred_element_type=jnp.float32).astype(
        jnp.bfloat16
    )
    bwd_received, grad_received = (
        lax.all_to_all(bwd_packed, "expert", split_axis=0, concat_axis=0, tiled=True),
        lax.all_to_all(grad_packed, "expert", split_axis=0, concat_axis=0, tiled=True),
    )
    bwd_slots = by_expert(bwd_received, expert_group, local_experts, capacity)
    grad_slots = by_expert(grad_received, expert_group, local_experts, capacity)
    partial_value = jnp.einsum(
        "erd,edf->erf", fwd_slots, up_local, preferred_element_type=jnp.float32
    )
    hidden = lax.psum_scatter(partial_value, "shard", scatter_dimension=2, tiled=True)
    active_part = jax.nn.silu(hidden).astype(jnp.bfloat16)
    active = lax.all_gather(active_part, "shard", axis=2, tiled=True)
    fwd_results = jnp.einsum(
        "erf,efd->erd", active, down_local, preferred_element_type=jnp.float32
    ).astype(jnp.bfloat16)
    fwd_returned = lax.all_to_all(
        by_source(fwd_results, expert_group, local_experts, capacity),
        "expert",
        split_axis=0,
        concat_axis=0,
        tiled=True,
    )
    layer_out = mix_rows(fwd_rows, fwd_targets, weight_fwd[0], fwd_returned)
    fwd_out = from_behind(layer_out, "section", 1)
    partial_hidden = jnp.einsum(
        "erd,edf->erf", bwd_slots, up_local, preferred_element_type=jnp.float32
    )
    partial_slope = jnp.einsum(
        "erd,efd->erf", grad_slots, down_local, preferred_element_type=jnp.float32
    )
    back_hidden, slope_in = (
        lax.psum_scatter(partial_hidden, "shard", scatter_dimension=2, tiled=True),
        lax.psum_scatter(partial_slope, "shard", scatter_dimension=2, tiled=True),
    )
    squash = jax.nn.sigmoid(back_hidden)
    slope_part = (slope_in * squash * (1.0 + back_hidden * (1.0 - squash))).astype(jnp.bfloat16)
    slope = lax.all_gather(slope_part, "shard", axis=2, tiled=True)
    bwd_results = jnp.einsum(
        "erf,edf->erd", slope, up_local, preferred_element_type=jnp.float32
    ).astype(jnp.bfloat16)
    bwd_returned = lax.all_to_all(
        by_source(bwd_results, expert_group, local_experts, capacity),
        "expert",
        split_axis=0,
        concat_axis=0,
        tiled=True,
    )
    layer_grad = mix_rows(grad_rows, bwd_targets, weight_bwd[0], bwd_returned)
    bwd_out = from_behind(layer_grad, "section", -1)
    return (fwd_out[None], bwd_out[None])


def solution(mesh):
    in_specs = (
        P("section", "expert", "shard"),
        P("section", "expert", "shard"),
        P("section", "expert", "shard"),
        P("section", "expert", "shard", None),
        P("section", "expert", None, "shard"),
        P("section", "expert", None),
        P("section", "expert", None),
        P("section", "expert", None),
        P("section", "expert", None),
    )
    out_specs = (P("section", "expert", "shard"), P("section", "expert", "shard"))
    return jax.shard_map(
        per_device, mesh=mesh, in_specs=in_specs, out_specs=out_specs, check_vma=False
    )
```

profile of v0, /device:TPU:0, one launch (start us, length us, event | category | flops | bytes accessed | tf_op | source)
XLA Modules:
  0.0 170.8 jit_solution(2826965592475642650)
XLA Ops:
  7.2 0.0 reduce-scatter.6.cloned.1.call-start
  7.2 0.9 copy.36
  8.1 0.1 eq.131
  8.3 0.1 eq.127
  8.4 1.2 reduce-window.16
  9.7 0.1 slice.39
  9.7 0.1 copy.39
  9.9 0.1 copy.40
  10.0 0.1 add_bitcast_fusion
  10.1 0.1 reduce_sum.49
  10.2 0.2 slice_reduce_fusion.1
  10.4 1.3 convolution_convert_fusion.1
  11.8 21.7 %all_to_all.51 = bf16[4,80,896]{2,1,0:T(8,128)(2,1)S(1)} all-to-all(bf16[4,80,896]{2,1,0:T(8,128)(2,1)S(1)} %bitcast.122), channel_id=1, replica_groups=mesh['section'=2,'expert'=4,'shard'=4] {'expert'}, dimensions={0} | all-to-all | bytes 1146880 | tf_op jit(solution)/shard_map/all_to_all | solution.py:80
  33.5 2.0 %fusion.16 = f32[1,320,1024]{2,1,0:T(8,128)} fusion(bf16[320,896]{1,0:T(8,128)(2,1)S(1)} %bitcast.123, bf16[1,1,1024,896]{3,2,1,0:T(8,128)(2,1)S(1)} %copy-done.8), kind=kOutput, calls=%fused_computation.14 | convolution fusion | flops 587202560 | bytes 3719168 | tf_op jit(solution)/shard_map/erd,efd->erf/dot_general | solution.py:105
  35.4 0.0 reduce-scatter.6.cloned.1.call-update
  35.5 0.0 reduce-scatter.8.cloned.1.call-start
  35.5 0.3 convolution_convert_fusion
  35.8 17.4 %all_to_all.52 = bf16[4,80,896]{2,1,0:T(8,128)(2,1)S(1)} all-to-all(bf16[4,80,896]{2,1,0:T(8,128)(2,1)S(1)} %bitcast.120), channel_id=1, replica_groups=mesh['section'=2,'expert'=4,'shard'=4] {'expert'}, dimensions={0} | all-to-all | bytes 1146880 | tf_op jit(solution)/shard_map/all_to_all | solution.py:79
  53.2 1.9 %fusion.13 = f32[1,320,1024]{2,1,0:T(8,128)} fusion(bf16[320,896]{1,0:T(8,128)(2,1)S(1)} %bitcast.124, bf16[1,1,896,1024]{3,2,1,0:T(8,128)(2,1)S(1)} %copy-done), kind=kOutput, calls=%fused_computation.13 | convolution fusion | flops 587202560 | bytes 3719168 | tf_op jit(solution)/shard_map/erd,edf->erf/dot_general | solution.py:102
  55.2 0.0 reduce-scatter.4.cloned.1.call-start
  55.3 0.1 copy.30
  55.4 0.1 eq.115
  55.5 0.1 eq.111
  55.7 1.2 reduce-window.14
  56.9 0.1 slice.36
  57.0 0.1 copy.33
  57.1 0.1 copy.34
  57.2 0.1 add_bitcast_fusion.1
  57.3 0.1 reduce_sum.45
  57.5 0.2 slice_reduce_fusion.3
  57.7 0.3 convolution_convert_fusion.2
  58.0 17.3 %all_to_all.53 = bf16[4,80,896]{2,1,0:T(8,128)(2,1)S(1)} all-to-all(bf16[4,80,896]{2,1,0:T(8,128)(2,1)S(1)} %bitcast.121), channel_id=1, replica_groups=mesh['section'=2,'expert'=4,'shard'=4] {'expert'}, dimensions={0} | all-to-all | bytes 1146880 | tf_op jit(solution)/shard_map/all_to_all | solution.py:68
  75.3 1.9 %fusion.10 = f32[1,320,1024]{2,1,0:T(8,128)} fusion(bf16[320,896]{1,0:T(8,128)(2,1)S(1)} %bitcast.125, bf16[1,1,896,1024]{3,2,1,0:T(8,128)(2,1)S(1)} %copy-done), kind=kOutput, calls=%fused_computation.12 | convolution fusion | flops 587202560 | bytes 3719168 | tf_op jit(solution)/shard_map/erd,edf->erf/dot_general | solution.py:84
  77.2 0.1 reduce_sum.50
  77.4 0.1 reduce_sum.46
  77.6 0.0 reduce-scatter.6.cloned.1.call-done
  77.6 12.6 %reduce-scatter.8.cloned.1.call-done = f32[1,320,256]{2,1,0:T(8,128)} async-done(((f32[1,320,1024]{2,1,0:T(8,128)}), f32[1,320,256]{2,1,0:T(8,128)}) %reduce-scatter.8.cloned.1.call-update) | async-done | bytes 327696 | tf_op jit(solution)/shard_map/reduce_scatter | solution.py:109
  90.2 1.2 multiply_convert_fusion
  91.4 7.3 %all_gather.7 = bf16[1,320,1024]{2,1,0:T(8,128)(2,1)S(1)} all-gather(bf16[1,320,256]{2,1,0:T(8,128)(2,1)S(1)} %multiply_convert_fusion), channel_id=1, replica_groups=mesh['section'=2,'expert'=4,'shard'=4] {'shard'}, dimensions={2}, use_global_device_ids=true | all-gather | bytes 819200 | tf_op jit(solution)/shard_map/all_gather | solution.py:114
  98.7 1.7 %fusion.19 = bf16[320,896]{1,0:T(8,128)(2,1)} fusion(bf16[1,1,896,1024]{3,2,1,0:T(8,128)(2,1)S(1)} %copy-done, bf16[1,320,1024]{2,1,0:T(8,128)(2,1)S(1)} %all_gather.7), kind=kOutput, calls=%fused_computation.15 | convolution fusion | flops 587489280 | bytes 3063808 | tf_op jit(solution)/shard_map/erf,edf->erd/dot_general | solution.py:115
  100.4 4.7 %all-to-all-start.4 = ((bf16[4,80,896]{2,1,0:T(8,128)(2,1)}), bf16[4,80,896]{2,1,0:T(8,128)(2,1)S(1)}, u32[]{:S(2)}, u32[]{:S(2)}) async-start(bf16[4,80,896]{2,1,0:T(8,128)(2,1)} %bitcast.28), calls=%async_computation.7 | async-start | bytes 1146880 | tf_op jit(solution)/shard_map/all_to_all | solution.py:118
  105.0 0.1 reshape.207
  105.2 0.7 copy.35
  105.9 0.1 reshape.199
  106.1 13.1 %reduce-scatter.4.cloned.1.call-done = f32[1,320,256]{2,1,0:T(8,128)} async-done(((f32[1,320,1024]{2,1,0:T(8,128)}), f32[1,320,256]{2,1,0:T(8,128)}) %reduce-scatter.4.cloned.1.call-update) | async-done | bytes 327696 | tf_op jit(solution)/shard_map/reduce_scatter | solution.py:87
  119.2 1.1 multiply_convert_fusion.1
  120.2 7.3 %all_gather.6 = bf16[1,320,1024]{2,1,0:T(8,128)(2,1)S(1)} all-gather(bf16[1,320,256]{2,1,0:T(8,128)(2,1)S(1)} %multiply_convert_fusion.1), channel_id=1, replica_groups=mesh['section'=2,'expert'=4,'shard'=4] {'shard'}, dimensions={2}, use_global_device_ids=true | all-gather | bytes 819200 | tf_op jit(solution)/shard_map/all_gather | solution.py:89
  127.5 3.2 %fusion.22 = bf16[320,896]{1,0:T(8,128)(2,1)} fusion(bf16[1,1,1024,896]{3,2,1,0:T(8,128)(2,1)} %param.13, bf16[1,320,1024]{2,1,0:T(8,128)(2,1)S(1)} %all_gather.6), kind=kOutput, calls=%fused_computation.16 | convolution fusion | flops 587489280 | bytes 3063808 | tf_op jit(solution)/shard_map/erf,efd->erd/dot_general | solution.py:90
  130.7 4.6 %all-to-all-start.1 = ((bf16[4,80,896]{2,1,0:T(8,128)(2,1)}), bf16[4,80,896]{2,1,0:T(8,128)(2,1)S(1)}, u32[]{:S(2)}, u32[]{:S(2)}) async-start(bf16[4,80,896]{2,1,0:T(8,128)(2,1)} %bitcast.11), calls=%async_computation.2 | async-start | bytes 1146880 | tf_op jit(solution)/shard_map/all_to_all | solution.py:93
  135.3 0.7 copy.29
  136.1 1.2 gather_fusion.1
  137.3 1.4 reshape.216
  138.7 2.4 %multiply_reduce_fusion = f32[128,896]{1,0:T(8,128)S(1)} fusion(f32[128,2,896]{2,1,0:T(2,128)} %reshape.216, f32[128,2]{1,0:T(8,128)} %copy.35), kind=kLoop, calls=%fused_computation.20 | loop fusion | flops 344064 | bytes 1377280 | tf_op jit(solution)/shard_map/reduce_sum | solution.py:46
  141.1 0.7 add_convert_fusion
  141.8 1.4 collective-permute-start.1
  143.3 8.1 %all-to-all-done.1 = bf16[4,80,896]{2,1,0:T(8,128)(2,1)S(1)} async-done(((bf16[4,80,896]{2,1,0:T(8,128)(2,1)}), bf16[4,80,896]{2,1,0:T(8,128)(2,1)S(1)}, u32[]{:S(2)}, u32[]{:S(2)}) %all-to-all-start.1) | async-done | bytes 573472 | tf_op jit(solution)/shard_map/all_to_all | solution.py:93
  151.4 1.2 gather_fusion
  152.6 0.4 reshape.215
  153.1 2.0 %multiply_reduce_fusion.1 = f32[128,896]{1,0:T(8,128)S(1)} fusion(f32[128,2,896]{2,1,0:T(2,128)S(1)} %reshape.215, f32[128,2]{1,0:T(8,128)} %copy.29), kind=kLoop, calls=%fused_computation.21 | loop fusion | flops 344064 | bytes 1377280 | tf_op jit(solution)/shard_map/reduce_sum | solution.py:46
  155.1 0.1 add_convert_fusion.1
  155.2 1.5 collective-permute-start
  156.7 5.3 %collective-permute-done = bf16[128,896]{1,0:T(8,128)(2,1)S(1)} collective-permute-done((bf16[128,896]{1,0:T(8,128)(2,1)S(1)}, bf16[128,896]{1,0:T(8,128)(2,1)S(1)}, u32[]{:S(2)}, u32[]{:S(2)}) %collective-permute-start) | collective-permute-done | bytes 229408 | tf_op jit(solution)/shard_map/ppermute | solution.py:10
  161.9 0.7 copy.47
  162.6 1.6 copy.48
  (38 shorter events, 0.3 us)
Async XLA Ops:
  7.2 46.1 %copy-start = (bf16[1,1,896,1024]{3,2,1,0:T(8,128)(2,1)S(1)}, bf16[1,1,896,1024]{3,2,1,0:T(8,128)(2,1)}, u32[]{:S(2)}) copy-start(bf16[1,1,896,1024]{3,2,1,0:T(8,128)(2,1)} %param.12) | copy-start | bytes 5505028
  7.2 70.4 %reduce-scatter.6.cloned.1.call-start = ((), (), s32[]{:S(2)}) async-start(), calls=%async_computation.9 | async-start | bytes 1638400 | tf_op jit(solution)/shard_map/reduce_scatter | solution.py:110
  10.2 23.3 %copy-start.8 = (bf16[1,1,1024,896]{3,2,1,0:T(8,128)(2,1)S(1)}, bf16[1,1,1024,896]{3,2,1,0:T(8,128)(2,1)}, u32[]{:S(2)}) copy-start(bf16[1,1,1024,896]{3,2,1,0:T(8,128)(2,1)} %param.13) | copy-start | bytes 5505028
  33.5 2.0 %copy-start.4 = (bf16[1,128,896]{2,1,0:T(8,128)(2,1)S(1)}, bf16[1,128,896]{2,1,0:T(8,128)(2,1)}, u32[]{:S(2)}) copy-start(bf16[1,128,896]{2,1,0:T(8,128)(2,1)} %param.10) | copy-start | bytes 688132
  35.5 54.7 %reduce-scatter.8.cloned.1.call-start = ((), (), s32[]{:S(2)}) async-start(), calls=%async_computation.10 | async-start | bytes 1638400 | tf_op jit(solution)/shard_map/reduce_scatter | solution.py:109
  53.2 2.0 %copy-start.5 = (s32[1,128,2]{1,2,0:T(2,128)S(1)}, s32[1,128,2]{1,2,0:T(2,128)}, u32[]{:S(2)}) copy-start(s32[1,128,2]{1,2,0:T(2,128)} %param.14) | copy-start | bytes 3076
  55.2 2.5 %copy-start.2 = (bf16[1,128,896]{2,1,0:T(8,128)(2,1)S(1)}, bf16[1,128,896]{2,1,0:T(8,128)(2,1)}, u32[]{:S(2)}) copy-start(bf16[1,128,896]{2,1,0:T(8,128)(2,1)} %param.9) | copy-start | bytes 688132
  55.2 64.0 %reduce-scatter.4.cloned.1.call-start = ((), (), s32[]{:S(2)}) async-start(), calls=%async_computation.8 | async-start | bytes 1638400 | tf_op jit(solution)/shard_map/reduce_scatter | solution.py:87
  98.7 6.4 %copy-start.6 = (s32[1,128,2]{1,2,0:T(2,128)S(1)}, s32[1,128,2]{1,2,0:T(2,128)}, u32[]{:S(2)}) copy-start(s32[1,128,2]{1,2,0:T(2,128)} %param.17) | copy-start | bytes 3076
  100.4 30.3 %all-to-all-start.4 = ((bf16[4,80,896]{2,1,0:T(8,128)(2,1)}), bf16[4,80,896]{2,1,0:T(8,128)(2,1)S(1)}, u32[]{:S(2)}, u32[]{:S(2)}) async-start(bf16[4,80,896]{2,1,0:T(8,128)(2,1)} %bitcast.28), calls=%async_computation.7 | async-start | bytes 1146880 | tf_op jit(solution)/shard_map/all_to_all | solution.py:118
  127.5 7.8 %copy-start.7 = (s32[1,128,2]{1,2,0:T(2,128)S(1)}, s32[1,128,2]{1,2,0:T(2,128)}, u32[]{:S(2)}) copy-start(s32[1,128,2]{1,2,0:T(2,128)} %param.15) | copy-start | bytes 3076
  130.7 20.7 %all-to-all-start.1 = ((bf16[4,80,896]{2,1,0:T(8,128)(2,1)}), bf16[4,80,896]{2,1,0:T(8,128)(2,1)S(1)}, u32[]{:S(2)}, u32[]{:S(2)}) async-start(bf16[4,80,896]{2,1,0:T(8,128)(2,1)} %bitcast.11), calls=%async_computation.2 | async-start | bytes 1146880 | tf_op jit(solution)/shard_map/all_to_all | solution.py:93
  137.3 3.8 %copy-start.1 = (bf16[1,128,896]{2,1,0:T(8,128)(2,1)S(1)}, bf16[1,128,896]{2,1,0:T(8,128)(2,1)}, u32[]{:S(2)}) copy-start(bf16[1,128,896]{2,1,0:T(8,128)(2,1)} %param.11) | copy-start | bytes 688132
  141.8 14.9 %collective-permute-start.1 = (bf16[128,896]{1,0:T(8,128)(2,1)}, bf16[128,896]{1,0:T(8,128)(2,1)}, u32[]{:S(2)}, u32[]{:S(2)}) collective-permute-start(bf16[128,896]{1,0:T(8,128)(2,1)} %add_convert_fusion), channel_id=1, source_target_pairs={{0,16},{16,0},{1,17},{17,1},{2,18},{18,2},{3,19},{19,3},{4,20},{20... | collective-permute-start | bytes 688136 | tf_op jit(solution)/shard_map/ppermute | solution.py:10
  152.6 2.5 %copy-start.3 = (bf16[1,128,896]{2,1,0:T(8,128)(2,1)S(1)}, bf16[1,128,896]{2,1,0:T(8,128)(2,1)}, u32[]{:S(2)}) copy-start(bf16[1,128,896]{2,1,0:T(8,128)(2,1)} %param.9) | copy-start | bytes 688132
  155.2 6.8 %collective-permute-start = (bf16[128,896]{1,0:T(8,128)(2,1)S(1)}, bf16[128,896]{1,0:T(8,128)(2,1)S(1)}, u32[]{:S(2)}, u32[]{:S(2)}) collective-permute-start(bf16[128,896]{1,0:T(8,128)(2,1)S(1)} %add_convert_fusion.1), channel_id=1, source_target_pairs={{0,16},{16,0},{1,17},{17,1},{2,18},{18,2},{3,19},{19,3},{4,20},{20... | collective-permute-start | bytes 688136 | tf_op jit(solution)/shard_map/ppermute | solution.py:10
Sparse Core Ops, SparseCore 0:
  35.6 25.5 reduce-scatter.5
  63.7 26.4 reduce-scatter.7
  92.7 26.4 reduce-scatter.3
where the time goes:
time: 171 us
  blocking collectives  71 us (42%)
  waiting for transfers between devices  39.2 us (23%)
  between operations  14 us (8%)
  matrix products  12.6 us (7%)
  starting transfers between devices  12.4 us (7%)
  local copies, waits for them, and re-layouts  11.4 us (7%)
  other arithmetic  10.2 us (6%)
    all_to_all x1, blocking collectives, per_device(): lax.all_to_all(grad_packed, 'expert', split_axis=0, concat_axis=0, tiled=...  21.7 us
    all_to_all x1, blocking collectives, per_device(): lax.all_to_all(bwd_packed, 'expert', split_axis=0, concat_axis=0, tiled=T...  17.4 us
    all_to_all x1, blocking collectives, per_device(): lax.all_to_all(fwd_packed, 'expert', split_axis=0, concat_axis=0, tiled=T...  17.3 us
    reduce_scatter x1, waiting for transfers between devices, per_device(): lax.psum_scatter(partial_value, 'shard', scatter_dimension=2, tiled=True)  13.1 us
    reduce_scatter x1, waiting for transfers between devices, per_device(): lax.psum_scatter(partial_hidden, 'shard', scatter_dimension=2, tiled=True)  12.6 us
    all_to_all x1, waiting for transfers between devices, per_device(): lax.all_to_all(by_source(fwd_results, expert_group, local_experts, capaci...  8.14 us
    all_gather x1, blocking collectives, per_device(): active = lax.all_gather(active_part, 'shard', axis=2, tiled=True)  7.3 us
    all_gather x1, blocking collectives, per_device(): slope = lax.all_gather(slope_part, 'shard', axis=2, tiled=True)  7.3 us
  transfers between devices with their start and end apart: 7, of which 4 were waited for; matrix products, arithmetic and copies ran while one was open for 15% of the time, Pallas kernels for 0%

commit v1 on v0

v1 whole, which is shorter than its diff:
```python
import functools

import jax
import jax.numpy as jnp
from jax import lax
from jax.experimental import pallas as pl
from jax.experimental.pallas import tpu as pltpu
from jax.sharding import PartitionSpec as P

MESH = pl.DeviceIdType.MESH
LANES = 128
ROWS = 16


def column_chunks(features):
    chunks, start = [], 0
    while start < features:
        size = min(3 * LANES, features - start)
        chunks.append((start, size))
        start += size
    return chunks


def kernel(dims, meta, fwd_in, saved_in, grad_in, w_in_hbm, w_out_hbm, fwd_out, bwd_out,
           w_in, w_out, pick, mix_hi, mix_lo, packed, slots, part_out, part_in, act,
           ret_out, ret_in, done, w_sem, disp_s, disp_r, part_s, part_r, act_s, act_r,
           ret_s, ret_r, hop_s, hop_r):
    sections, group, shards, cap, tokens, features, quarter, groups = dims
    per_group = group // groups
    span = per_group * cap
    chunks = column_chunks(features)
    sec = lax.axis_index("section")
    me = lax.axis_index("expert")
    mine = lax.axis_index("shard")

    load_in = pltpu.make_async_copy(w_in_hbm.at[0, 0], w_in, w_sem.at[0])
    load_out = pltpu.make_async_copy(w_out_hbm.at[0, 0], w_out, w_sem.at[1])
    load_in.start()
    load_out.start()

    def expert_peer(k):
        return (sec, lax.rem(me + k, group), mine)

    def shard_peer(k):
        return (sec, me, lax.rem(mine + k, shards))

    def section_peer(k):
        return (lax.rem(sec + k + sections, sections), me, mine)

    barrier = pltpu.get_barrier_semaphore()
    peers = [expert_peer(k) for k in range(1, group)]
    peers += [shard_peer(k) for k in range(1, shards)]
    peers += [section_peer(1), section_peer(-1)]
    for peer in peers:
        pl.semaphore_signal(barrier, inc=1, device_id=peer, device_id_type=MESH)

    upper = (lax.broadcasted_iota(jnp.int32, (tokens, tokens), 0)
             < lax.broadcasted_iota(jnp.int32, (tokens, tokens), 1)).astype(jnp.bfloat16)
    height = max(group, 8)
    labels = lax.rem(lax.broadcasted_iota(jnp.int32, (height, tokens), 0) + me, group)
    spots = lax.broadcasted_iota(jnp.int32, (cap, tokens), 0)
    for way in range(2):
        base = 4 * way
        first = jnp.broadcast_to(meta[base : base + 1, :], (height, tokens)) == labels
        second = jnp.broadcast_to(meta[base + 1 : base + 2, :], (height, tokens)) == labels
        q_first = jnp.broadcast_to(meta[base + 2 : base + 3, :], (height, tokens))
        q_second = jnp.broadcast_to(meta[base + 3 : base + 4, :], (height, tokens))
        weight = jnp.where(first, q_first, 0) + jnp.where(second, q_second, 0)
        named = jnp.where(first, 1, 0) + jnp.where(second, 1, 0)
        rank = jnp.dot(named.astype(jnp.float32).astype(jnp.bfloat16), upper,
                       preferred_element_type=jnp.float32).astype(jnp.int32)
        spot = jnp.where(named > 0, rank, cap)
        high = weight >> 8
        low = weight & 255
        for k in range(group):
            hit = jnp.broadcast_to(spot[k : k + 1, :], (cap, tokens)) == spots
            rows = pl.ds(k * cap, cap)
            pick[way, rows, :] = jnp.where(hit, 1.0, 0.0).astype(jnp.bfloat16)
            mix_hi[way, rows, :] = jnp.where(
                hit, jnp.broadcast_to(high[k : k + 1, :], (cap, tokens)), 0
            ).astype(jnp.float32).astype(jnp.bfloat16)
            mix_lo[way, rows, :] = jnp.where(
                hit, jnp.broadcast_to(low[k : k + 1, :], (cap, tokens)), 0
            ).astype(jnp.float32).astype(jnp.bfloat16)

    pending = []
    sources = (fwd_in, saved_in, grad_in)

    def dispatch(t, k):
        return pltpu.make_async_remote_copy(
            src_ref=packed.at[t, pl.ds(k * cap, cap)],
            dst_ref=slots.at[t, pl.ds(k * cap, cap)],
            send_sem=disp_s.at[t, k],
            recv_sem=disp_r.at[t, k],
            device_id=expert_peer(k),
            device_id_type=MESH,
        )

    def pack(t):
        way = 0 if t == 0 else 1
        rows = jnp.dot(pick[way], sources[t][0], preferred_element_type=jnp.float32)
        rows = rows.astype(jnp.bfloat16)
        slots[t, pl.ds(0, cap), :] = rows[:cap]
        packed[t, pl.ds(cap, (group - 1) * cap), :] = rows[cap:]

    pack(1)
    pack(2)
    pl.semaphore_wait(barrier, len(peers))
    for k in range(1, group):
        for t in (1, 2):
            copy = dispatch(t, k)
            copy.start()
            pending.append(copy)
    pack(0)
    for k in range(1, group):
        copy = dispatch(0, k)
        copy.start()
        pending.append(copy)

    def part_copy(t, g, k):
        peer = lax.rem(mine + k, shards)
        return pltpu.make_async_remote_copy(
            src_ref=part_out.at[t, peer, pl.ds(g * span, span)],
            dst_ref=part_in.at[t, k - 1, pl.ds(g * span, span)],
            send_sem=part_s.at[t, g, k - 1],
            recv_sem=part_r.at[t, g, k - 1],
            device_id=shard_peer(k),
            device_id_type=MESH,
        )

    def act_copy(way, g, k):
        return pltpu.make_async_remote_copy(
            src_ref=act.at[way, mine, pl.ds(g * span, span)],
            dst_ref=act.at[way, mine, pl.ds(g * span, span)],
            send_sem=act_s.at[way, g, k - 1],
            recv_sem=act_r.at[way, g, k - 1],
            device_id=shard_peer(k),
            device_id_type=MESH,
        )

    def send_parts(t, g):
        for k in range(1, shards):
            copy = part_copy(t, g, k)
            copy.start()
            pending.append(copy)

    def arrive(t, g):
        for b in range(per_group):
            k = g * per_group + b
            if k > 0:
                dispatch(t, k).wait_recv()

    def partial(t, g):
        rows = pl.ds(g * span, span)
        arrive(t, g)

        @pl.loop(0, shards)
        def _(q):
            cols = pl.ds(pl.multiple_of(q * quarter, quarter), quarter)
            if t == 2:
                value = lax.dot_general(
                    slots[t, rows, :], w_out[cols, :], (((1,), (1,)), ((), ())),
                    preferred_element_type=jnp.float32)
            else:
                value = jnp.dot(slots[t, rows, :], w_in[:, cols],
                                preferred_element_type=jnp.float32)
            part_out[t, q, rows, :] = value.astype(jnp.bfloat16)

        send_parts(t, g)

    def total(t, g):
        rows = pl.ds(g * span, span)
        value = part_out[t, mine, rows, :].astype(jnp.float32)
        for k in range(1, shards):
            part_copy(t, g, k).wait_recv()
            value = value + part_in[t, k - 1, rows, :].astype(jnp.float32)
        return value

    def send_act(way, g, value):
        act[way, mine, pl.ds(g * span, span), :] = value.astype(jnp.bfloat16)
        for k in range(1, shards):
            copy = act_copy(way, g, k)
            copy.start()
            pending.append(copy)

    def forward_act(g):
        hidden = total(0, g)
        send_act(0, g, hidden / (1.0 + jnp.exp(-hidden)))

    def backward_act(g):
        hidden = total(1, g)
        slope = total(2, g)
        squash = 1.0 / (1.0 + jnp.exp(-hidden))
        send_act(1, g, slope * squash * (1.0 + hidden * (1.0 - squash)))

    def ret_copy(way, c, k):
        start, size = chunks[c]
        view = (way, pl.ds(k * cap, cap), pl.ds(start, size))
        return pltpu.make_async_remote_copy(
            src_ref=ret_out.at[view],
            dst_ref=ret_in.at[view],
            send_sem=ret_s.at[way, c, k],
            recv_sem=ret_r.at[way, c, k],
            device_id=(sec, lax.rem(me - k + group, group), mine),
            device_id_type=MESH,
        )

    def give_back(way):
        for g in range(groups):
            for k in range(1, shards):
                act_copy(way, g, k).wait_recv()
        for c, (start, size) in enumerate(chunks):
            cols = pl.ds(start, size)
            value = None
            for q in range(shards):
                units = pl.ds(q * quarter, quarter)
                if way == 0:
                    term = jnp.dot(act[way, q], w_out[units, cols],
                                   preferred_element_type=jnp.float32)
                else:
                    term = lax.dot_general(
                        act[way, q], w_in[cols, units], (((1,), (1,)), ((), ())),
                        preferred_element_type=jnp.float32)
                value = term if value is None else value + term
            value = value.astype(jnp.bfloat16)
            ret_in[way, pl.ds(0, cap), cols] = value[:cap]
            ret_out[way, pl.ds(cap, (group - 1) * cap), cols] = value[cap:]
            for k in range(1, group):
                copy = ret_copy(way, c, k)
                copy.start()
                pending.append(copy)

    def hop_copy(way, c):
        start, size = chunks[c]
        out = fwd_out if way == 0 else bwd_out
        return pltpu.make_async_remote_copy(
            src_ref=done.at[way, :, pl.ds(start, size)],
            dst_ref=out.at[0, :, pl.ds(start, size)],
            send_sem=hop_s.at[way, c],
            recv_sem=hop_r.at[way, c],
            device_id=section_peer(1 if way == 0 else -1),
            device_id_type=MESH,
        )

    def mix(way):
        tok = fwd_in if way == 0 else grad_in
        over = (((0,), (0,)), ((), ()))
        for c, (start, size) in enumerate(chunks):
            cols = pl.ds(start, size)
            for k in range(1, group):
                ret_copy(way, c, k).wait_recv()
            back = ret_in[way, :, cols]
            high = lax.dot_general(mix_hi[way], back, over, preferred_element_type=jnp.float32)
            low = lax.dot_general(mix_lo[way], back, over, preferred_element_type=jnp.float32)
            summed = (high * 256.0 + low) * (1.0 / 32768.0)
            done[way, :, cols] = (tok[0, :, cols].astype(jnp.float32) + summed).astype(
                jnp.bfloat16)
            copy = hop_copy(way, c)
            copy.start()
            pending.append(copy)

    load_in.wait()
    load_out.wait()
    last = groups - 1
    for g in range(groups):
        partial(1, g)
        partial(2, g)
        if g < last:
            backward_act(g)
    partial(0, 0)
    backward_act(last)
    if groups > 1:
        partial(0, 1)
    give_back(1)
    forward_act(0)
    for g in range(2, groups):
        partial(0, g)
        forward_act(g - 1)
    if groups > 1:
        forward_act(last)
    give_back(0)
    mix(1)
    mix(0)
    for way in (1, 0):
        for c in range(len(chunks)):
            hop_copy(way, c).wait_recv()
    for copy in pending:
        copy.wait_send()


def per_device(dims_base, fwd_in, saved_in, grad_in, w_in, w_out, ids_fwd, weight_fwd, ids_bwd,
               weight_bwd):
    sections, group, shards = dims_base
    tokens, features = fwd_in.shape[1:]
    hidden = w_in.shape[3]
    assert w_in.shape[:2] == (1, 1)
    top = ids_fwd.shape[2]
    assert top == 2
    room = max(2, (tokens * top * 5 + 4 * group - 1) // (4 * group))
    cap = -(-room // ROWS) * ROWS
    groups = 4 if group % 4 == 0 else 1
    quarter = hidden // shards
    rows = group * cap
    nc = len(column_chunks(features))
    dims = (sections, group, shards, cap, tokens, features, quarter, groups)
    meta = jnp.concatenate(
        [ids_fwd[0].T, weight_fwd[0].T, ids_bwd[0].T, weight_bwd[0].T], axis=0)
    bf = jnp.bfloat16
    dma = pltpu.SemaphoreType.DMA
    vmem = pl.BlockSpec(memory_space=pltpu.VMEM)
    anywhere = pl.BlockSpec(memory_space=pl.ANY)
    out = jax.ShapeDtypeStruct(fwd_in.shape, bf)
    return pl.pallas_call(
        functools.partial(kernel, dims),
        name="relay",
        out_shape=(out, out),
        in_specs=[vmem] * 4 + [anywhere] * 2,
        out_specs=(vmem, vmem),
        scratch_shapes=[
            pltpu.VMEM((features, hidden), bf),
            pltpu.VMEM((hidden, features), bf),
            pltpu.VMEM((2, rows, tokens), bf),
            pltpu.VMEM((2, rows, tokens), bf),
            pltpu.VMEM((2, rows, tokens), bf),
            pltpu.VMEM((3, rows, features), bf),
            pltpu.VMEM((3, rows, features), bf),
            pltpu.VMEM((3, shards, rows, quarter), bf),
            pltpu.VMEM((3, shards - 1, rows, quarter), bf),
            pltpu.VMEM((2, shards, rows, quarter), bf),
            pltpu.VMEM((2, rows, features), bf),
            pltpu.VMEM((2, rows, features), bf),
            pltpu.VMEM((2, tokens, features), bf),
            dma((2,)),
            dma((3, group)), dma((3, group)),
            dma((3, groups, shards - 1)), dma((3, groups, shards - 1)),
            dma((2, groups, shards - 1)), dma((2, groups, shards - 1)),
            dma((2, nc, group)), dma((2, nc, group)),
            dma((2, nc)), dma((2, nc)),
        ],
        compiler_params=pltpu.CompilerParams(
            collective_id=0, has_side_effects=True, vmem_limit_bytes=56 * 2**20),
    )(meta, fwd_in, saved_in, grad_in, w_in, w_out)


def solution(mesh):
    rows = P("section", "expert", "shard")
    slots = P("section", "expert", None)
    dims_base = (mesh.shape["section"], mesh.shape["expert"], mesh.shape["shard"])
    return jax.shard_map(
        functools.partial(per_device, dims_base),
        mesh=mesh,
        in_specs=(rows, rows, rows, P("section", "expert", "shard", None),
                  P("section", "expert", None, "shard"), slots, slots, slots, slots),
        out_specs=(rows, rows),
        check_vma=False,
    )
```

time: 171 us -> 95 us (0.56)
  Pallas kernels: 0 us -> 89.5 us
  blocking collectives: 71 us -> 0 us
  waiting for transfers between devices: 39.2 us -> 0 us
  between operations: 14 us -> 0.64 us
  matrix products: 12.6 us -> 0 us
  starting transfers between devices: 12.4 us -> 0 us
  other arithmetic: 10.2 us -> 1.33 us
  local copies, waits for them, and re-layouts: 11.4 us -> 3.29 us
    pallas_call x0 -> x1, Pallas kernels: none -> 89.5 us  [per_device(): pl.pallas_call(functools.partial(kernel, dims), name='relay', out_shape=(...]
    all_to_all x3 -> x0, blocking collectives: 56.4 us -> none  [the longest x1 21.7 us: per_device(): lax.all_to_all(grad_packed, 'expert', split_axis=0, concat_axis=0, tiled=...]
    reduce_scatter x3 -> x0, waiting for transfers between devices: 25.7 us -> none  [the longest x1 13.1 us: per_device(): lax.psum_scatter(partial_value, 'shard', scatter_dimension=2, tiled=True)]
    all_gather x2 -> x0, blocking collectives: 14.6 us -> none  [the longest x1 7.3 us: per_device(): active = lax.all_gather(active_part, 'shard', axis=2, tiled=True)]
    dot_general x8 -> x0, matrix products: 12.6 us -> none  [the longest x1 3.17 us: per_device(): jnp.einsum('erf,efd->erd', active, down_local, preferred_element_type=jnp...]
    all_to_all x2 -> x0, starting transfers between devices: 9.28 us -> none  [the longest x1 4.66 us: per_device(): lax.all_to_all(by_source(bwd_results, expert_group, local_experts, capaci...]
    all_to_all x2 -> x0, waiting for transfers between devices: 8.15 us -> none  [the longest x1 8.14 us: per_device(): lax.all_to_all(by_source(fwd_results, expert_group, local_experts, capaci...]
    ppermute x2 -> x0, waiting for transfers between devices: 5.28 us -> none  [from_behind(): return lax.ppermute(value, axis, pairs)]
  transfers between devices with their start and end apart: 7 -> 0, of which waited for: 4 -> 0; matrix products, arithmetic and copies ran while one was open for 15% -> 0% of each run, Pallas kernels for 0% -> 0%
where the time goes in v1:
time: 95 us; the launch traced here: 94.8 us
  Pallas kernels  89.5 us (94%)
  local copies, waits for them, and re-layouts  3.29 us (3%)
  other arithmetic  1.33 us (1%)
    pallas_call x1, Pallas kernels, per_device(): pl.pallas_call(functools.partial(kernel, dims), name='relay', out_shape=(...  89.5 us
    unnamed x2, local copies, waits for them, and re-layouts  3.29 us

profile of v1, /device:TPU:0, one launch (start us, length us, event | category | flops | bytes accessed | tf_op | source)
XLA Modules:
  0.0 94.8 jit_solution(17313413956796491115)
XLA Ops:
  0.6 1.3 %pad_add_fusion.meta = s32[8,128]{1,0:T(8,128)} fusion(s32[2,128]{1,0:T(2,128)} %bitcast.12, s32[2,128]{1,0:T(2,128)} %bitcast.13, s32[2,128]{1,0:T(2,128)} %bitcast.14, s32[2,128]{1,0:T(2,128)} %bitcast.15), kind=kLoop, calls=%fused_computation | loop fusion | flops 3072 | bytes 8192 | tf_op jit(solution)/shard_map/concatenate | solution.py:306
  2.0 89.5 %relay.1 = (bf16[1,128,896]{2,1,0:T(8,128)(2,1)}, bf16[1,128,896]{2,1,0:T(8,128)(2,1)}) custom-call(s32[8,128]{1,0:T(8,128)} %pad_add_fusion.meta, bf16[1,128,896]{2,1,0:T(8,128)(2,1)} %fwd_in.1, bf16[1,128,896]{2,1,0:T(8,128)(2,1)} %saved_in.1, bf16[1,128,896]{2,1,0:T(8,128)(2,1)} %grad_in.1, bf16[1,1,896,1024]{3,2,1,0:T(8,128)(2,1)} %w_in_hbm.1, ...), custom_call_target="tpu_custom_call" | custom-call | tf_op jit(solution)/shard_map/relay/pallas_call | solution.py:313
  91.5 1.6 %copy.13 = bf16[1,128,896]{2,1,0:T(8,128)(2,1)} copy(bf16[1,128,896]{2,1,0:T(8,128)(2,1)} %get-tuple-element.4) | data formatting | bytes 458752
  93.1 1.6 %copy.14 = bf16[1,128,896]{2,1,0:T(8,128)(2,1)} copy(bf16[1,128,896]{2,1,0:T(8,128)(2,1)} %get-tuple-element.5) | data formatting | bytes 458752

commit v2 on v1

--- a/solution.py
+++ b/solution.py
@@ -103,19 +103,27 @@
         slots[t, pl.ds(0, cap), :] = rows[:cap]
         packed[t, pl.ds(cap, (group - 1) * cap), :] = rows[cap:]
 
+    def blocks(g):
+        return [k for k in range(g * per_group, (g + 1) * per_group) if k > 0]
+
+    def issue(tensors, g):
+        for k in blocks(g):
+            for t in tensors:
+                dispatch(t, k).start()
+
+    def drain(tensors, g):
+        for k in blocks(g):
+            for t in tensors:
+                dispatch(t, k).wait_send()
+
     pack(1)
     pack(2)
     pl.semaphore_wait(barrier, len(peers))
-    for k in range(1, group):
-        for t in (1, 2):
-            copy = dispatch(t, k)
-            copy.start()
-            pending.append(copy)
+    queue = [(t, g) for t in ((1, 2), (0,)) for g in range(groups) if blocks(g)]
+    sent = min(2, len(queue))
+    for item in queue[:sent]:
+        issue(*item)
     pack(0)
-    for k in range(1, group):
-        copy = dispatch(0, k)
-        copy.start()
-        pending.append(copy)
 
     def part_copy(t, g, k):
         peer = lax.rem(mine + k, shards)
@@ -205,7 +213,7 @@
             device_id_type=MESH,
         )
 
-    def give_back(way):
+    def give_back(way, ahead):
         for g in range(groups):
             for k in range(1, shards):
                 act_copy(way, g, k).wait_recv()
@@ -226,9 +234,11 @@
             ret_in[way, pl.ds(0, cap), cols] = value[:cap]
             ret_out[way, pl.ds(cap, (group - 1) * cap), cols] = value[cap:]
             for k in range(1, group):
-                copy = ret_copy(way, c, k)
-                copy.start()
-                pending.append(copy)
+                if c >= ahead:
+                    ret_copy(way, c - ahead, k).wait_send()
+                ret_copy(way, c, k).start()
+        for c in range(max(0, len(chunks) - ahead), len(chunks)):
+            pending.extend(ret_copy(way, c, k) for k in range(1, group))
 
     def hop_copy(way, c):
         start, size = chunks[c]
@@ -265,20 +275,28 @@
     for g in range(groups):
         partial(1, g)
         partial(2, g)
+        drain((1, 2), g)
+        if blocks(g) and sent < len(queue):
+            issue(*queue[sent])
+            sent += 1
         if g < last:
             backward_act(g)
+    for item in queue[sent:]:
+        issue(*item)
     partial(0, 0)
     backward_act(last)
     if groups > 1:
         partial(0, 1)
-    give_back(1)
+    give_back(1, len(chunks))
     forward_act(0)
     for g in range(2, groups):
         partial(0, g)
         forward_act(g - 1)
     if groups > 1:
         forward_act(last)
-    give_back(0)
+    for g in range(groups):
+        drain((0,), g)
+    give_back(0, 2)
     mix(1)
     mix(0)
     for way in (1, 0):
@@ -286,6 +304,20 @@
             hop_copy(way, c).wait_recv()
     for copy in pending:
         copy.wait_send()
+
+
+def settle(fwd, bwd, fwd_out, bwd_out, rows, sem):
+    loads = [pltpu.make_async_copy(ref, rows.at[i], sem.at[0, i])
+             for i, ref in enumerate((fwd, bwd))]
+    stores = [pltpu.make_async_copy(rows.at[i], ref, sem.at[1, i])
+              for i, ref in enumerate((fwd_out, bwd_out))]
+    for load in loads:
+        load.start()
+    for load, store in zip(loads, stores):
+        load.wait()
+        store.start()
+    for store in stores:
+        store.wait()
 
 
 def per_device(dims_base, fwd_in, saved_in, grad_in, w_in, w_out, ids_fwd, weight_fwd, ids_bwd,
@@ -310,7 +342,7 @@
     vmem = pl.BlockSpec(memory_space=pltpu.VMEM)
     anywhere = pl.BlockSpec(memory_space=pl.ANY)
     out = jax.ShapeDtypeStruct(fwd_in.shape, bf)
-    return pl.pallas_call(
+    fwd, bwd = pl.pallas_call(
         functools.partial(kernel, dims),
         name="relay",
         out_shape=(out, out),
@@ -340,6 +372,14 @@
         compiler_params=pltpu.CompilerParams(
             collective_id=0, has_side_effects=True, vmem_limit_bytes=56 * 2**20),
     )(meta, fwd_in, saved_in, grad_in, w_in, w_out)
+    return pl.pallas_call(
+        settle,
+        name="settle",
+        out_shape=(out, out),
+        in_specs=[anywhere] * 2,
+        out_specs=(anywhere, anywhere),
+        scratch_shapes=[pltpu.VMEM((2,) + fwd_in.shape, bf), dma((2, 2))],
+    )(fwd, bwd)
 
 
 def solution(mesh):

time: 95 us -> 89.9 us (0.946)
  local copies, waits for them, and re-layouts: 3.29 us -> 0 us
  Pallas kernels: 89.5 us -> 87.8 us
    pallas_call x1, Pallas kernels: 89.5 us -> 86 us  [per_device(): pl.pallas_call(functools.partial(kernel, dims), name='relay', out_shape=(...]
    unnamed x2 -> x0, local copies, waits for them, and re-layouts: 3.29 us -> none
    pallas_call x0 -> x1, Pallas kernels: none -> 1.77 us  [per_device(): pl.pallas_call(settle, name='settle', out_shape=(out, out), in_specs=[any...]
where the time goes in v2:
time: 89.9 us; the launch traced here: 89.8 us
  Pallas kernels  87.8 us (98%)
  other arithmetic  1.33 us (1%)
    pallas_call x1, Pallas kernels, per_device(): pl.pallas_call(functools.partial(kernel, dims), name='relay', out_shape=(...  86 us

profile of v2, /device:TPU:0, one launch (start us, length us, event | category | flops | bytes accessed | tf_op | source)
XLA Modules:
  0.0 89.8 jit_solution(9789260525865930249)
XLA Ops:
  0.6 1.3 %pad_add_fusion.meta = s32[8,128]{1,0:T(8,128)} fusion(s32[2,128]{1,0:T(2,128)} %bitcast.12, s32[2,128]{1,0:T(2,128)} %bitcast.13, s32[2,128]{1,0:T(2,128)} %bitcast.14, s32[2,128]{1,0:T(2,128)} %bitcast.15), kind=kLoop, calls=%fused_computation | loop fusion | flops 3072 | bytes 8192 | tf_op jit(solution)/shard_map/concatenate | solution.py:338
  2.0 86.0 %relay.1 = (bf16[1,128,896]{2,1,0:T(8,128)(2,1)}, bf16[1,128,896]{2,1,0:T(8,128)(2,1)}) custom-call(s32[8,128]{1,0:T(8,128)} %pad_add_fusion.meta, bf16[1,128,896]{2,1,0:T(8,128)(2,1)} %fwd_in.1, bf16[1,128,896]{2,1,0:T(8,128)(2,1)} %saved_in.1, bf16[1,128,896]{2,1,0:T(8,128)(2,1)} %grad_in.1, bf16[1,1,896,1024]{3,2,1,0:T(8,128)(2,1)} %w_in_hbm.1, ...), custom_call_target="tpu_custom_call" | custom-call | tf_op jit(solution)/shard_map/relay/pallas_call | solution.py:345
  88.0 1.8 %settle.1 = (bf16[1,128,896]{2,1,0:T(8,128)(2,1)}, bf16[1,128,896]{2,1,0:T(8,128)(2,1)}) custom-call(bf16[1,128,896]{2,1,0:T(8,128)(2,1)} %get-tuple-element.4.fwd, bf16[1,128,896]{2,1,0:T(8,128)(2,1)} %get-tuple-element.5.bwd), custom_call_target="tpu_custom_call" | custom-call | tf_op jit(solution)/shard_map/settle/pallas_call | solution.py:375

commit v3 on v2

--- a/solution.py
+++ b/solution.py
@@ -15,13 +15,13 @@
 def column_chunks(features):
     chunks, start = [], 0
     while start < features:
-        size = min(3 * LANES, features - start)
+        size = min(2 * LANES, features - start)
         chunks.append((start, size))
         start += size
     return chunks
 
 
-def kernel(dims, meta, fwd_in, saved_in, grad_in, w_in_hbm, w_out_hbm, fwd_out, bwd_out,
+def kernel(dims, ids_fwd, q_fwd, ids_bwd, q_bwd, fwd_in, saved_in, grad_in, w_in_hbm, w_out_hbm, fwd_out, bwd_out,
            w_in, w_out, pick, mix_hi, mix_lo, packed, slots, part_out, part_in, act,
            ret_out, ret_in, done, w_sem, disp_s, disp_r, part_s, part_r, act_s, act_r,
            ret_s, ret_r, hop_s, hop_r):
@@ -59,29 +59,33 @@
     height = max(group, 8)
     labels = lax.rem(lax.broadcasted_iota(jnp.int32, (height, tokens), 0) + me, group)
     spots = lax.broadcasted_iota(jnp.int32, (cap, tokens), 0)
-    for way in range(2):
-        base = 4 * way
-        first = jnp.broadcast_to(meta[base : base + 1, :], (height, tokens)) == labels
-        second = jnp.broadcast_to(meta[base + 1 : base + 2, :], (height, tokens)) == labels
-        q_first = jnp.broadcast_to(meta[base + 2 : base + 3, :], (height, tokens))
-        q_second = jnp.broadcast_to(meta[base + 3 : base + 4, :], (height, tokens))
-        weight = jnp.where(first, q_first, 0) + jnp.where(second, q_second, 0)
+    over = (height, tokens)
+
+    def find(way):
+        ids = ids_fwd if way == 0 else ids_bwd
+        first = jnp.broadcast_to(ids[0:1, :], over) == labels
+        second = jnp.broadcast_to(ids[1:2, :], over) == labels
         named = jnp.where(first, 1, 0) + jnp.where(second, 1, 0)
         rank = jnp.dot(named.astype(jnp.float32).astype(jnp.bfloat16), upper,
                        preferred_element_type=jnp.float32).astype(jnp.int32)
         spot = jnp.where(named > 0, rank, cap)
-        high = weight >> 8
-        low = weight & 255
         for k in range(group):
             hit = jnp.broadcast_to(spot[k : k + 1, :], (cap, tokens)) == spots
+            pick[way, pl.ds(k * cap, cap), :] = jnp.where(hit, 1.0, 0.0).astype(jnp.bfloat16)
+        return first, second
+
+    def weigh(way, found):
+        first, second = found
+        q = q_fwd if way == 0 else q_bwd
+        weight = jnp.where(first, jnp.broadcast_to(q[0:1, :], over), 0) + jnp.where(
+            second, jnp.broadcast_to(q[1:2, :], over), 0)
+        high = (weight >> 8).astype(jnp.float32).astype(jnp.bfloat16)
+        low = (weight & 255).astype(jnp.float32).astype(jnp.bfloat16)
+        for k in range(group):
             rows = pl.ds(k * cap, cap)
-            pick[way, rows, :] = jnp.where(hit, 1.0, 0.0).astype(jnp.bfloat16)
-            mix_hi[way, rows, :] = jnp.where(
-                hit, jnp.broadcast_to(high[k : k + 1, :], (cap, tokens)), 0
-            ).astype(jnp.float32).astype(jnp.bfloat16)
-            mix_lo[way, rows, :] = jnp.where(
-                hit, jnp.broadcast_to(low[k : k + 1, :], (cap, tokens)), 0
-            ).astype(jnp.float32).astype(jnp.bfloat16)
+            hit = pick[way, rows, :]
+            mix_hi[way, rows, :] = hit * jnp.broadcast_to(high[k : k + 1, :], (cap, tokens))
+            mix_lo[way, rows, :] = hit * jnp.broadcast_to(low[k : k + 1, :], (cap, tokens))
 
     pending = []
     sources = (fwd_in, saved_in, grad_in)
@@ -116,6 +120,7 @@
             for t in tensors:
                 dispatch(t, k).wait_send()
 
+    found_bwd = find(1)
     pack(1)
     pack(2)
     pl.semaphore_wait(barrier, len(peers))
@@ -123,7 +128,10 @@
     sent = min(2, len(queue))
     for item in queue[:sent]:
         issue(*item)
+    found_fwd = find(0)
     pack(0)
+    weigh(1, found_bwd)
+    weigh(0, found_fwd)
 
     def part_copy(t, g, k):
         peer = lax.rem(mine + k, shards)
@@ -202,7 +210,7 @@
         send_act(1, g, slope * squash * (1.0 + hidden * (1.0 - squash)))
 
     def ret_copy(way, c, k):
-        start, size = chunks[c]
+        start, size = chunks[c] if way == 0 else (0, features)
         view = (way, pl.ds(k * cap, cap), pl.ds(start, size))
         return pltpu.make_async_remote_copy(
             src_ref=ret_out.at[view],
@@ -213,32 +221,51 @@
             device_id_type=MESH,
         )
 
-    def give_back(way, ahead):
+    def rows_back(g):
+        for k in range(1, shards):
+            act_copy(1, g, k).wait_recv()
+        value = None
+        for q in range(shards):
+            term = lax.dot_general(
+                act[1, q, pl.ds(g * span, span), :], w_in[:, pl.ds(q * quarter, quarter)],
+                (((1,), (1,)), ((), ())), preferred_element_type=jnp.float32)
+            value = term if value is None else value + term
+        value = value.astype(jnp.bfloat16)
+        for b in range(per_group):
+            k = g * per_group + b
+            target = ret_in if k == 0 else ret_out
+            target[1, pl.ds(k * cap, cap), :] = value[b * cap : (b + 1) * cap]
+
+    def send_back(g):
+        for k in blocks(g):
+            copy = ret_copy(1, 0, k)
+            copy.start()
+            pending.append(copy)
+
+    def give_back(ahead):
         for g in range(groups):
             for k in range(1, shards):
-                act_copy(way, g, k).wait_recv()
+                act_copy(0, g, k).wait_recv()
         for c, (start, size) in enumerate(chunks):
             cols = pl.ds(start, size)
             value = None
             for q in range(shards):
-                units = pl.ds(q * quarter, quarter)
-                if way == 0:
-                    term = jnp.dot(act[way, q], w_out[units, cols],
-                                   preferred_element_type=jnp.float32)
-                else:
-                    term = lax.dot_general(
-                        act[way, q], w_in[cols, units], (((1,), (1,)), ((), ())),
-                        preferred_element_type=jnp.float32)
+                term = jnp.dot(act[0, q], w_out[pl.ds(q * quarter, quarter), cols],
+                               preferred_element_type=jnp.float32)
                 value = term if value is None else value + term
             value = value.astype(jnp.bfloat16)
-            ret_in[way, pl.ds(0, cap), cols] = value[:cap]
-            ret_out[way, pl.ds(cap, (group - 1) * cap), cols] = value[cap:]
+            ret_in[0, pl.ds(0, cap), cols] = value[:cap]
+            ret_out[0, pl.ds(cap, (group - 1) * cap), cols] = value[cap:]
+            if c < ahead:
+                for k in range(1, group):
+                    ret_copy(0, c, k).start()
+
+    def follow(c):
+        for k in range(1, group):
+            ret_copy(0, c, k).wait_send()
+        if c + 2 < len(chunks):
             for k in range(1, group):
-                if c >= ahead:
-                    ret_copy(way, c - ahead, k).wait_send()
-                ret_copy(way, c, k).start()
-        for c in range(max(0, len(chunks) - ahead), len(chunks)):
-            pending.extend(ret_copy(way, c, k) for k in range(1, group))
+                ret_copy(0, c + 2, k).start()
 
     def hop_copy(way, c):
         start, size = chunks[c]
@@ -252,22 +279,22 @@
             device_id_type=MESH,
         )
 
-    def mix(way):
+    def mix(way, c):
         tok = fwd_in if way == 0 else grad_in
-        over = (((0,), (0,)), ((), ()))
-        for c, (start, size) in enumerate(chunks):
-            cols = pl.ds(start, size)
+        across = (((0,), (0,)), ((), ()))
+        start, size = chunks[c]
+        cols = pl.ds(start, size)
+        if way == 0 or c == 0:
             for k in range(1, group):
                 ret_copy(way, c, k).wait_recv()
-            back = ret_in[way, :, cols]
-            high = lax.dot_general(mix_hi[way], back, over, preferred_element_type=jnp.float32)
-            low = lax.dot_general(mix_lo[way], back, over, preferred_element_type=jnp.float32)
-            summed = (high * 256.0 + low) * (1.0 / 32768.0)
-            done[way, :, cols] = (tok[0, :, cols].astype(jnp.float32) + summed).astype(
-                jnp.bfloat16)
-            copy = hop_copy(way, c)
-            copy.start()
-            pending.append(copy)
+        back = ret_in[way, :, cols]
+        high = lax.dot_general(mix_hi[way], back, across, preferred_element_type=jnp.float32)
+        low = lax.dot_general(mix_lo[way], back, across, preferred_element_type=jnp.float32)
+        summed = (high * 256.0 + low) * (1.0 / 32768.0)
+        done[way, :, cols] = (tok[0, :, cols].astype(jnp.float32) + summed).astype(jnp.bfloat16)
+        copy = hop_copy(way, c)
+        copy.start()
+        pending.append(copy)
 
     load_in.wait()
     load_out.wait()
@@ -281,24 +308,30 @@
             sent += 1
         if g < last:
             backward_act(g)
+            if g > 0:
+                rows_back(g - 1)
     for item in queue[sent:]:
         issue(*item)
     partial(0, 0)
     backward_act(last)
-    if groups > 1:
-        partial(0, 1)
-    give_back(1, len(chunks))
-    forward_act(0)
-    for g in range(2, groups):
-        partial(0, g)
-        forward_act(g - 1)
-    if groups > 1:
-        forward_act(last)
+    if last > 0:
+        rows_back(last - 1)
     for g in range(groups):
+        if g > 0:
+            partial(0, g)
         drain((0,), g)
-    give_back(0, 2)
-    mix(1)
-    mix(0)
+        if g > 0:
+            send_back(g - 1)
+            forward_act(g - 1)
+    rows_back(last)
+    send_back(last)
+    forward_act(last)
+    give_back(2)
+    for c in range(len(chunks)):
+        mix(1, c)
+    for c in range(len(chunks)):
+        follow(c)
+        mix(0, c)
     for way in (1, 0):
         for c in range(len(chunks)):
             hop_copy(way, c).wait_recv()
@@ -335,8 +368,7 @@
     rows = group * cap
     nc = len(column_chunks(features))
     dims = (sections, group, shards, cap, tokens, features, quarter, groups)
-    meta = jnp.concatenate(
-        [ids_fwd[0].T, weight_fwd[0].T, ids_bwd[0].T, weight_bwd[0].T], axis=0)
+    routing = [a[0].T for a in (ids_fwd, weight_fwd, ids_bwd, weight_bwd)]
     bf = jnp.bfloat16
     dma = pltpu.SemaphoreType.DMA
     vmem = pl.BlockSpec(memory_space=pltpu.VMEM)
@@ -346,7 +378,7 @@
         functools.partial(kernel, dims),
         name="relay",
         out_shape=(out, out),
-        in_specs=[vmem] * 4 + [anywhere] * 2,
+        in_specs=[vmem] * 7 + [anywhere] * 2,
         out_specs=(vmem, vmem),
         scratch_shapes=[
             pltpu.VMEM((features, hidden), bf),
@@ -371,7 +403,7 @@
         ],
         compiler_params=pltpu.CompilerParams(
             collective_id=0, has_side_effects=True, vmem_limit_bytes=56 * 2**20),
-    )(meta, fwd_in, saved_in, grad_in, w_in, w_out)
+    )(*routing, fwd_in, saved_in, grad_in, w_in, w_out)
     return pl.pallas_call(
         settle,
         name="settle",

time: 89.9 us -> 86.8 us (0.966)
  Pallas kernels: 87.8 us -> 86 us
  other arithmetic: 1.33 us -> 0 us
    pallas_call x1, Pallas kernels: 86 us -> 84.2 us  [per_device(): pl.pallas_call(functools.partial(kernel, dims), name='relay', out_shape=(...]
    concatenate x1 -> x0, other arithmetic: 1.33 us -> none  [per_device(): jnp.concatenate([ids_fwd[0].T, weight_fwd[0].T, ids_bwd[0].T, weight_bwd[...]
where the time goes in v3:
time: 86.8 us; the launch traced here: 86.6 us
  Pallas kernels  86 us (99%)
    pallas_call x1, Pallas kernels, per_device(): pl.pallas_call(functools.partial(kernel, dims), name='relay', out_shape=(...  84.2 us
    pallas_call x1, Pallas kernels, per_device(): pl.pallas_call(settle, name='settle', out_shape=(out, out), in_specs=[any...  1.77 us

profile of v3, /device:TPU:0, one launch (start us, length us, event | category | flops | bytes accessed | tf_op | source)
XLA Modules:
  0.0 86.6 jit_solution(2854600855888590975)
XLA Ops:
  0.6 84.2 %relay.1 = (bf16[1,128,896]{2,1,0:T(8,128)(2,1)}, bf16[1,128,896]{2,1,0:T(8,128)(2,1)}) custom-call(s32[2,128]{1,0:T(2,128)} %bitcast.12, s32[2,128]{1,0:T(2,128)} %bitcast.13, s32[2,128]{1,0:T(2,128)} %bitcast.14, s32[2,128]{1,0:T(2,128)} %bitcast.15, bf16[1,128,896]{2,1,0:T(8,128)(2,1)} %fwd_in.1, bf16[1,128,896]{2,1,0:T(8,128)(2,1)} %saved_in.1, ...), custom_call_target="tpu_custom_call" | custom-call | tf_op jit(solution)/shard_map/relay/pallas_call | solution.py:377
  84.8 1.8 %settle.1 = (bf16[1,128,896]{2,1,0:T(8,128)(2,1)}, bf16[1,128,896]{2,1,0:T(8,128)(2,1)}) custom-call(bf16[1,128,896]{2,1,0:T(8,128)(2,1)} %get-tuple-element.4.fwd, bf16[1,128,896]{2,1,0:T(8,128)(2,1)} %get-tuple-element.5.bwd), custom_call_target="tpu_custom_call" | custom-call | tf_op jit(solution)/shard_map/settle/pallas_call | solution.py:407

commit v4 on v3

--- a/solution.py
+++ b/solution.py
@@ -29,6 +29,7 @@
     per_group = group // groups
     span = per_group * cap
     chunks = column_chunks(features)
+    last = groups - 1
     sec = lax.axis_index("section")
     me = lax.axis_index("expert")
     mine = lax.axis_index("shard")
@@ -120,16 +121,16 @@
             for t in tensors:
                 dispatch(t, k).wait_send()
 
+    found_fwd = find(0)
+    pack(0)
+    pl.semaphore_wait(barrier, len(peers))
+    queue = [(t, g) for t in ((0,), (1, 2)) for g in range(groups) if blocks(g)]
+    sent = min(3, len(queue))
+    for item in queue[:sent]:
+        issue(*item)
     found_bwd = find(1)
     pack(1)
     pack(2)
-    pl.semaphore_wait(barrier, len(peers))
-    queue = [(t, g) for t in ((1, 2), (0,)) for g in range(groups) if blocks(g)]
-    sent = min(2, len(queue))
-    for item in queue[:sent]:
-        issue(*item)
-    found_fwd = find(0)
-    pack(0)
     weigh(1, found_bwd)
     weigh(0, found_fwd)
 
@@ -210,7 +211,8 @@
         send_act(1, g, slope * squash * (1.0 + hidden * (1.0 - squash)))
 
     def ret_copy(way, c, k):
-        start, size = chunks[c] if way == 0 else (0, features)
+        start, size = (0, features) if c is None else chunks[c]
+        c = 0 if c is None else c
         view = (way, pl.ds(k * cap, cap), pl.ds(start, size))
         return pltpu.make_async_remote_copy(
             src_ref=ret_out.at[view],
@@ -238,11 +240,11 @@
 
     def send_back(g):
         for k in blocks(g):
-            copy = ret_copy(1, 0, k)
+            copy = ret_copy(1, None, k)
             copy.start()
             pending.append(copy)
 
-    def give_back(ahead):
+    def give_back():
         for g in range(groups):
             for k in range(1, shards):
                 act_copy(0, g, k).wait_recv()
@@ -256,16 +258,23 @@
             value = value.astype(jnp.bfloat16)
             ret_in[0, pl.ds(0, cap), cols] = value[:cap]
             ret_out[0, pl.ds(cap, (group - 1) * cap), cols] = value[cap:]
-            if c < ahead:
-                for k in range(1, group):
-                    ret_copy(0, c, k).start()
+
+    def send_forward():
+        for c in range(len(chunks)):
+            for k in range(1, group):
+                copy = ret_copy(0, c, k)
+                copy.start()
+                pending.append(copy)
+
+    def send_last(c):
+        for k in blocks(last):
+            ret_copy(1, c, k).start()
 
     def follow(c):
-        for k in range(1, group):
-            ret_copy(0, c, k).wait_send()
+        for k in blocks(last):
+            ret_copy(1, c, k).wait_send()
         if c + 2 < len(chunks):
-            for k in range(1, group):
-                ret_copy(0, c + 2, k).start()
+            send_last(c + 2)
 
     def hop_copy(way, c):
         start, size = chunks[c]
@@ -284,9 +293,16 @@
         across = (((0,), (0,)), ((), ()))
         start, size = chunks[c]
         cols = pl.ds(start, size)
-        if way == 0 or c == 0:
+        if way == 0:
             for k in range(1, group):
-                ret_copy(way, c, k).wait_recv()
+                ret_copy(0, c, k).wait_recv()
+        else:
+            for g in range(groups):
+                for k in blocks(g):
+                    if g == last:
+                        ret_copy(1, c, k).wait_recv()
+                    elif c == 0:
+                        ret_copy(1, None, k).wait_recv()
         back = ret_in[way, :, cols]
         high = lax.dot_general(mix_hi[way], back, across, preferred_element_type=jnp.float32)
         low = lax.dot_general(mix_lo[way], back, across, preferred_element_type=jnp.float32)
@@ -298,40 +314,44 @@
 
     load_in.wait()
     load_out.wait()
-    last = groups - 1
+    for g in range(groups):
+        partial(0, g)
+        drain((0,), g)
+        if blocks(g) and sent < len(queue):
+            issue(*queue[sent])
+            sent += 1
+        if g > 0:
+            forward_act(g - 1)
+    for item in queue[sent:]:
+        issue(*item)
     for g in range(groups):
         partial(1, g)
         partial(2, g)
-        drain((1, 2), g)
-        if blocks(g) and sent < len(queue):
-            issue(*queue[sent])
-            sent += 1
+        if g == 0:
+            forward_act(last)
         if g < last:
             backward_act(g)
-            if g > 0:
-                rows_back(g - 1)
-    for item in queue[sent:]:
-        issue(*item)
-    partial(0, 0)
+        if g == 0:
+            give_back()
+        elif g < last:
+            rows_back(g - 1)
+    for g in range(groups):
+        drain((1, 2), g)
+    send_forward()
+    for g in range(last - 1):
+        send_back(g)
     backward_act(last)
     if last > 0:
         rows_back(last - 1)
-    for g in range(groups):
-        if g > 0:
-            partial(0, g)
-        drain((0,), g)
-        if g > 0:
-            send_back(g - 1)
-            forward_act(g - 1)
+        send_back(last - 1)
     rows_back(last)
-    send_back(last)
-    forward_act(last)
-    give_back(2)
+    for c in range(min(2, len(chunks))):
+        send_last(c)
     for c in range(len(chunks)):
-        mix(1, c)
+        mix(0, c)
     for c in range(len(chunks)):
         follow(c)
-        mix(0, c)
+        mix(1, c)
     for way in (1, 0):
         for c in range(len(chunks)):
             hop_copy(way, c).wait_recv()

time: 86.8 us -> 93.8 us (1.081)
  Pallas kernels: 86 us -> 93 us
    pallas_call x1, Pallas kernels: 84.2 us -> 91.2 us  [per_device(): pl.pallas_call(functools.partial(kernel, dims), name='relay', out_shape=(...]
where the time goes in v4:
time: 93.8 us; the launch traced here: 93.6 us
  Pallas kernels  93 us (99%)
    pallas_call x1, Pallas kernels, per_device(): pl.pallas_call(functools.partial(kernel, dims), name='relay', out_shape=(...  91.2 us

profile of v4, /device:TPU:0, one launch (start us, length us, event | category | flops | bytes accessed | tf_op | source)
XLA Modules:
  0.0 93.6 jit_solution(10241303698401630689)
XLA Ops:
  0.6 91.2 %relay.1 = (bf16[1,128,896]{2,1,0:T(8,128)(2,1)}, bf16[1,128,896]{2,1,0:T(8,128)(2,1)}) custom-call(s32[2,128]{1,0:T(2,128)} %bitcast.12, s32[2,128]{1,0:T(2,128)} %bitcast.13, s32[2,128]{1,0:T(2,128)} %bitcast.14, s32[2,128]{1,0:T(2,128)} %bitcast.15, bf16[1,128,896]{2,1,0:T(8,128)(2,1)} %fwd_in.1, bf16[1,128,896]{2,1,0:T(8,128)(2,1)} %saved_in.1, ...), custom_call_target="tpu_custom_call" | custom-call | tf_op jit(solution)/shard_map/relay/pallas_call | solution.py:397
  91.9 1.8 %settle.1 = (bf16[1,128,896]{2,1,0:T(8,128)(2,1)}, bf16[1,128,896]{2,1,0:T(8,128)(2,1)}) custom-call(bf16[1,128,896]{2,1,0:T(8,128)(2,1)} %get-tuple-element.4.fwd, bf16[1,128,896]{2,1,0:T(8,128)(2,1)} %get-tuple-element.5.bwd), custom_call_target="tpu_custom_call" | custom-call | tf_op jit(solution)/shard_map/settle/pallas_call | solution.py:427

commit v5 on v3

--- a/solution.py
+++ b/solution.py
@@ -125,7 +125,7 @@
     pack(2)
     pl.semaphore_wait(barrier, len(peers))
     queue = [(t, g) for t in ((1, 2), (0,)) for g in range(groups) if blocks(g)]
-    sent = min(2, len(queue))
+    sent = min(3, len(queue))
     for item in queue[:sent]:
         issue(*item)
     found_fwd = find(0)
@@ -242,7 +242,7 @@
             copy.start()
             pending.append(copy)
 
-    def give_back(ahead):
+    def give_back():
         for g in range(groups):
             for k in range(1, shards):
                 act_copy(0, g, k).wait_recv()
@@ -256,16 +256,10 @@
             value = value.astype(jnp.bfloat16)
             ret_in[0, pl.ds(0, cap), cols] = value[:cap]
             ret_out[0, pl.ds(cap, (group - 1) * cap), cols] = value[cap:]
-            if c < ahead:
-                for k in range(1, group):
-                    ret_copy(0, c, k).start()
-
-    def follow(c):
-        for k in range(1, group):
-            ret_copy(0, c, k).wait_send()
-        if c + 2 < len(chunks):
             for k in range(1, group):
-                ret_copy(0, c + 2, k).start()
+                copy = ret_copy(0, c, k)
+                copy.start()
+                pending.append(copy)
 
     def hop_copy(way, c):
         start, size = chunks[c]
@@ -326,11 +320,10 @@
     rows_back(last)
     send_back(last)
     forward_act(last)
-    give_back(2)
+    give_back()
     for c in range(len(chunks)):
         mix(1, c)
     for c in range(len(chunks)):
-        follow(c)
         mix(0, c)
     for way in (1, 0):
         for c in range(len(chunks)):

time: 86.8 us -> 86.1 us (level)
  no operation moved by 1% of the time
where the time goes in v5:
time: 86.1 us; the launch traced here: 86 us
  Pallas kernels  85.3 us (99%)
    pallas_call x1, Pallas kernels, per_device(): pl.pallas_call(functools.partial(kernel, dims), name='relay', out_shape=(...  83.6 us
    pallas_call x1, Pallas kernels, per_device(): pl.pallas_call(settle, name='settle', out_shape=(out, out), in_specs=[any...  1.77 us

profile of v5, /device:TPU:0, one launch (start us, length us, event | category | flops | bytes accessed | tf_op | source)
XLA Modules:
  0.0 86.0 jit_solution(17661436432434208122)
XLA Ops:
  0.6 83.6 %relay.1 = (bf16[1,128,896]{2,1,0:T(8,128)(2,1)}, bf16[1,128,896]{2,1,0:T(8,128)(2,1)}) custom-call(s32[2,128]{1,0:T(2,128)} %bitcast.12, s32[2,128]{1,0:T(2,128)} %bitcast.13, s32[2,128]{1,0:T(2,128)} %bitcast.14, s32[2,128]{1,0:T(2,128)} %bitcast.15, bf16[1,128,896]{2,1,0:T(8,128)(2,1)} %fwd_in.1, bf16[1,128,896]{2,1,0:T(8,128)(2,1)} %saved_in.1, ...), custom_call_target="tpu_custom_call" | custom-call | tf_op jit(solution)/shard_map/relay/pallas_call | solution.py:370
  84.2 1.8 %settle.1 = (bf16[1,128,896]{2,1,0:T(8,128)(2,1)}, bf16[1,128,896]{2,1,0:T(8,128)(2,1)}) custom-call(bf16[1,128,896]{2,1,0:T(8,128)(2,1)} %get-tuple-element.4.fwd, bf16[1,128,896]{2,1,0:T(8,128)(2,1)} %get-tuple-element.5.bwd), custom_call_target="tpu_custom_call" | custom-call | tf_op jit(solution)/shard_map/settle/pallas_call | solution.py:400
